TPU v7x, 512 devices: a whole 4x4x16 slice. The times are simulated.
512 devices in a mesh: lon: 64 (over z, x), lat: 8 (over y, core).
Axes of the slice: x: 4, y: 4, z: 16, core: 2. Of those that a mesh axis runs over, the one named last changes fastest.
Arguments:
- wet_mask: int32 [4096, 8192], P('lat', 'lon'), may hold values 0 or 1
- east_level: int32 [4096, 8192], P('lat', 'lon'), may hold values from 0 to 8
- north_level: int32 [4096, 8192], P('lat', 'lon'), may hold values from 0 to 8, as said below
- courant: float32 [4096, 8192], P('lat', 'lon'), may hold values from 0.1 to 0.45
- increment: float32 [4096, 8192], P('lat', 'lon'), may hold values from -6 to 6
- innovation: float32 [4096, 8192], P('lat', 'lon'), may hold values from -6 to 6
- obs_weight: float32 [4096, 8192], P('lat', 'lon'), may hold values from 0.2 to 2
- smooth_scale: float32 [4096], P('lat'), may hold values from 2.5 to 10
Outputs:
- final_eta: float32 [4096, 8192], P('lat', 'lon')
- precond_grad: float32 [4096, 8192], P('lat', 'lon')
Inputs may be any that keep to these rules, and one draw needn't show every extreme that they name: `north_level`: on the top row every north face is open at least half of 8 levels.
All inputs are finite; a program needn't handle non-finite values. No bound on the sum of `wet_mask` on one device may be relied on, other than what follows from the above.
Results may differ from a plain program's by a relative error of at most 0.00023.
Values sent between devices are 32-bit elements; how exact they have to be, the bound alone decides.
A program may use at most 64 MiB of HBM per device.

v0:
```python
import jax
import jax.numpy as jnp
from jax import lax
from jax.sharding import PartitionSpec as P

SUBSTEPS = 4
WLEV = 8


def with_halo(block, sides, width):
    for axis, dim in sides:
        count = lax.axis_size(axis)
        forward = [(i, i + 1) for i in range(count - 1)]
        forward.append((count - 1, 0))
        backward = [(target, source) for source, target in forward]
        low = lax.ppermute(
            lax.slice_in_dim(block, block.shape[dim] - width, None, axis=dim), axis, forward
        )
        high = lax.ppermute(lax.slice_in_dim(block, 0, width, axis=dim), axis, backward)
        block = jnp.concatenate([low, block, high], axis=dim)
    return block


def shifted(value, axis, steps):
    count = lax.axis_size(axis)
    pairs = [(source, (source + steps) % count) for source in range(count)]
    return lax.ppermute(value, axis, pairs)


def passed_along(value, axis, steps):
    count = lax.axis_size(axis)
    leading, last = (max(0, -steps), min(count, count - steps))
    return lax.ppermute(value, axis, [(source, source + steps) for source in range(leading, last)])


def shift_cols(values, stride, eastward):
    if eastward:
        return jnp.pad(values[..., :-stride], ((0, 0), (0, 0), (stride, 0)))
    return jnp.pad(values[..., stride:], ((0, 0), (0, 0), (0, stride)))


def block_cycle(east_end, west_end, block_decay):
    east_sum = east_end
    west_sum = west_end
    weight = block_decay
    blocks_all = east_end.shape[1]
    for bit_index in range(blocks_all.bit_length() - 1):
        stride = 2**bit_index
        east_sum = east_sum + weight * jnp.roll(east_sum, stride, axis=1)
        west_sum = west_sum + weight * jnp.roll(west_sum, -stride, axis=1)
        weight = weight * weight
    return (east_sum, west_sum, blocks_all)


def zonal_solve(source, stiffness, cycle):
    width = source.shape[-1]
    stiff_rows = stiffness[:, None, None]
    root_term = jnp.sqrt(1.0 + 4.0 * stiff_rows)
    log_root = jnp.log1p(-(root_term - 1.0) / (2.0 * stiff_rows))
    green_scale = 1.0 / root_term
    forward_sum = source
    backward_sum = source
    stride = 1
    while stride < width:
        factor = jnp.exp(float(stride) * log_root)
        forward_sum = forward_sum + factor * shift_cols(forward_sum, stride, True)
        backward_sum = backward_sum + factor * shift_cols(backward_sum, stride, False)
        stride = stride * 2
    row_log = log_root[..., 0]
    block_decay = jnp.exp(float(width) * row_log)
    east_end = forward_sum[..., -1]
    west_end = backward_sum[..., 0]
    east_sum, west_sum, blocks_all = cycle(east_end, west_end, block_decay)
    wrap_weight = jnp.exp(float((blocks_all - 1) * width) * row_log)
    image_sum = 1.0 - jnp.exp(float(blocks_all * width) * row_log)
    east_in = ((east_sum - east_end) / block_decay + wrap_weight * east_end) / image_sum
    west_in = ((west_sum - west_end) / block_decay + wrap_weight * west_end) / image_sum
    column = jnp.arange(width, dtype=jnp.float32)
    forward_all = forward_sum + jnp.exp((column + 1.0) * log_root) * east_in[..., None]
    backward_all = backward_sum + jnp.exp((float(width) - column) * log_root) * west_in[..., None]
    return green_scale * (forward_all + backward_all - source)


def mirror_row(values, col_count):
    gathered = lax.all_gather(values, "lon", axis=0, tiled=True)
    return lax.dynamic_slice_in_dim(gathered[::-1], lax.axis_index("lon") * col_count, col_count)


def laplace(state_now, face_set, at_top):
    east_face, west_face, north_face, south_face = face_set
    padded = with_halo(state_now, (("lat", 0), ("lon", 1)), 1)
    folded = mirror_row(state_now[-1], state_now.shape[1])
    north_vals = padded[2:, 1:-1]
    north_vals = north_vals.at[-1].set(jnp.where(at_top, folded, north_vals[-1]))
    return (
        east_face * (padded[1:-1, 2:] - state_now)
        + west_face * (padded[1:-1, :-2] - state_now)
        + north_face * (north_vals - state_now)
        + south_face * (padded[:-2, 1:-1] - state_now)
    )


def local(
    wet_mask, east_level, north_level, courant, increment, innovation, obs_weight, smooth_scale
):
    row_count, col_count = increment.shape
    lon_count = lax.axis_size("lon")
    at_top = lax.axis_index("lat") == lax.axis_size("lat") - 1
    wet_frac = wet_mask.astype(jnp.float32)
    east_face = east_level.astype(jnp.float32) / WLEV
    raw_north = north_level.astype(jnp.float32) / WLEV
    west_edge = shifted(east_face[:, -1], "lon", 1)
    west_face = jnp.concatenate([west_edge[:, None], east_face[:, :-1]], axis=1)
    south_edge = passed_along(raw_north[-1], "lat", 1)
    south_face = jnp.concatenate([south_edge[None], raw_north[:-1]], axis=0)
    top_faces = raw_north[-1]
    fold_face = top_faces * mirror_row(top_faces, col_count)
    north_face = raw_north.at[-1].set(jnp.where(at_top, fold_face, top_faces))
    face_set = (east_face, west_face, north_face, south_face)
    state_now = wet_frac * increment
    before = state_now
    for substep in range(SUBSTEPS):
        after = 2.0 * state_now - before + wet_frac * courant * laplace(state_now, face_set, at_top)
        before = state_now
        state_now = after
    adjoint = wet_frac * obs_weight * (state_now - innovation)
    carried = jnp.zeros_like(adjoint)
    for substep in range(SUBSTEPS):
        updated = (
            2.0 * adjoint
            + wet_frac * laplace(courant * wet_frac * adjoint, face_set, at_top)
            + carried
        )
        carried = -adjoint
        adjoint = updated
    gradient = wet_frac * (adjoint + carried)
    lines = lax.all_to_all(gradient, "lon", split_axis=0, concat_axis=1, tiled=True)
    line_rows = row_count // lon_count
    row_scales = lax.dynamic_slice_in_dim(
        smooth_scale, lax.axis_index("lon") * line_rows, line_rows
    )
    stiffness = row_scales * float(col_count * col_count)
    blocked = lines.reshape(line_rows, lon_count, col_count)
    smoothed = zonal_solve(blocked, stiffness, block_cycle).reshape(
        line_rows, lon_count * col_count
    )
    smoothed = smoothed * (2.0 * stiffness**0.25)[:, None]
    precond_grad = lax.all_to_all(smoothed, "lon", split_axis=1, concat_axis=0, tiled=True)
    return (state_now, precond_grad)


def solution(mesh):
    return jax.shard_map(
        local,
        mesh=mesh,
        in_specs=(
            P("lat", "lon"),
            P("lat", "lon"),
            P("lat", "lon"),
            P("lat", "lon"),
            P("lat", "lon"),
            P("lat", "lon"),
            P("lat", "lon"),
            P("lat"),
        ),
        out_specs=(P("lat", "lon"), P("lat", "lon")),
        check_vma=False,
    )
```

profile of v0, /device:TPU:2, one launch (start us, length us, event | category | flops | bytes accessed | tf_op | source)
XLA Modules:
  0.0 885.1 jit_solution(8038742436026527924)
XLA Ops:
  6.3 3.4 collective-permute-start.3
  9.7 79.2 %all-gather = f32[1,8192]{1,0:T(1,128)S(1)} all-gather(f32[1,128]{1,0:T(1,128)S(1)} %get-tuple-element.160), channel_id=2, replica_groups=mesh['lon'=64,'lat'=8] {'lon'}, dimensions={1}, use_global_device_ids=true | all-gather | bytes 33280 | tf_op jit(solution)/shard_map/all_gather | solution.py:85
  89.1 72.9 %all-gather.1 = f32[1,8192]{1,0:T(1,128)S(1)} all-gather(f32[1,128]{1,0:T(1,128)S(1)} %get-tuple-element.162), channel_id=3, replica_groups=mesh['lon'=64,'lat'=8] {'lon'}, dimensions={1}, use_global_device_ids=true | all-gather | bytes 33280 | tf_op jit(solution)/shard_map/all_gather | solution.py:85
  175.6 2.9 collective-permute-start.7
  178.5 75.9 %all-gather.2 = f32[1,8192]{1,0:T(1,128)S(1)} all-gather(f32[1,128]{1,0:T(1,128)S(1)} %get-tuple-element.158), channel_id=4, replica_groups=mesh['lon'=64,'lat'=8] {'lon'}, dimensions={1}, use_global_device_ids=true | all-gather | bytes 33280 | tf_op jit(solution)/shard_map/all_gather | solution.py:85
  257.4 3.9 collective-permute-start.8
  269.0 75.5 %all-gather.3 = f32[1,8192]{1,0:T(1,128)S(1)} all-gather(f32[1,128]{1,0:T(1,128)S(1)} %get-tuple-element.156), channel_id=5, replica_groups=mesh['lon'=64,'lat'=8] {'lon'}, dimensions={1}, use_global_device_ids=true | all-gather | bytes 33280 | tf_op jit(solution)/shard_map/all_gather | solution.py:85
  345.5 3.0 collective-permute-start.13
  360.2 75.6 %all-gather.4 = f32[1,8192]{1,0:T(1,128)S(1)} all-gather(f32[1,128]{1,0:T(1,128)S(1)} %get-tuple-element.154), channel_id=6, replica_groups=mesh['lon'=64,'lat'=8] {'lon'}, dimensions={1}, use_global_device_ids=true | all-gather | bytes 33280 | tf_op jit(solution)/shard_map/all_gather | solution.py:85
  438.7 3.9 collective-permute-start.16
  449.3 3.0 collective-permute-start.19
  452.3 76.7 %all-gather.5 = f32[1,8192]{1,0:T(1,128)S(1)} all-gather(f32[1,128]{1,0:T(1,128)S(1)} %get-tuple-element.152), channel_id=7, replica_groups=mesh['lon'=64,'lat'=8] {'lon'}, dimensions={1}, use_global_device_ids=true | all-gather | bytes 33280 | tf_op jit(solution)/shard_map/all_gather | solution.py:85
  529.2 3.0 collective-permute-start.21
  537.5 3.1 collective-permute-done.20
  544.9 75.6 %all-gather.6 = f32[1,8192]{1,0:T(1,128)S(1)} all-gather(f32[1,128]{1,0:T(1,128)S(1)} %get-tuple-element.150), channel_id=8, replica_groups=mesh['lon'=64,'lat'=8] {'lon'}, dimensions={1}, use_global_device_ids=true | all-gather | bytes 33280 | tf_op jit(solution)/shard_map/all_gather | solution.py:85
  623.4 3.9 collective-permute-start.24
  636.4 75.5 %all-gather.7 = f32[1,8192]{1,0:T(1,128)S(1)} all-gather(f32[1,128]{1,0:T(1,128)S(1)} %get-tuple-element.148), channel_id=9, replica_groups=mesh['lon'=64,'lat'=8] {'lon'}, dimensions={1}, use_global_device_ids=true | all-gather | bytes 33280 | tf_op jit(solution)/shard_map/all_gather | solution.py:85
  712.9 3.0 collective-permute-start.29
  721.4 3.1 collective-permute-done.28
  728.8 75.6 %all-gather.8 = f32[1,8192]{1,0:T(1,128)S(1)} all-gather(f32[1,128]{1,0:T(1,128)S(1)} %get-tuple-element.146), channel_id=10, replica_groups=mesh['lon'=64,'lat'=8] {'lon'}, dimensions={1}, use_global_device_ids=true | all-gather | bytes 33280 | tf_op jit(solution)/shard_map/all_gather | solution.py:85
  807.3 3.9 collective-permute-start.32
  817.0 17.4 %all-to-all-start = ((f32[64,8,128]{2,1,0:T(8,128)}), f32[64,8,128]{2,1,0:T(8,128)S(1)}, u32[]{:S(2)}, u32[]{:S(2)}) async-start(f32[64,8,128]{2,1,0:T(8,128)} %fusion.9), calls=%async_computation | async-start | bytes 524288 | tf_op jit(solution)/shard_map/all_to_all | solution.py:137
  835.4 21.2 %all-to-all-done = f32[64,8,128]{2,1,0:T(8,128)S(1)} async-done(((f32[64,8,128]{2,1,0:T(8,128)}), f32[64,8,128]{2,1,0:T(8,128)S(1)}, u32[]{:S(2)}, u32[]{:S(2)}) %all-to-all-start) | async-done | bytes 262176 | tf_op jit(solution)/shard_map/all_to_all | solution.py:137
  860.6 23.8 %all_to_all.32 = f32[8,64,128]{2,0,1:T(8,128)S(1)} all-to-all(f32[8,64,128]{2,0,1:T(8,128)S(1)} %copy.746), channel_id=1, replica_groups=mesh['lon'=64,'lat'=8] {'lon'}, dimensions={1} | all-to-all | bytes 524288 | tf_op jit(solution)/shard_map/all_to_all | solution.py:148
  (195 shorter events, 99.1 us)
Async XLA Ops:
  1.8 160.3 %collective-permute-start = (f32[1,128]{1,0:T(1,128)S(1)}, f32[1,128]{1,0:T(1,128)S(1)}, u32[]{:S(2)}, u32[]{:S(2)}) collective-permute-start(f32[1,128]{1,0:T(1,128)S(1)} %get-tuple-element.162), channel_id=1, source_target_pairs={{0,1},{1,2},{2,3},{3,4},{4,5},{5,6},{6,7},{7,0},{8,9},{9,10},{10,1... | collective-permute-start | bytes 1544 | tf_op jit(solution)/shard_map/ppermute | solution.py:16
  1.8 160.3 %collective-permute-start.1 = (f32[1,128]{1,0:T(1,128)S(1)}, f32[1,128]{1,0:T(1,128)S(1)}, u32[]{:S(2)}, u32[]{:S(2)}) collective-permute-start(f32[1,128]{1,0:T(1,128)S(1)} %get-tuple-element.161), channel_id=1, source_target_pairs={{1,0},{2,1},{3,2},{4,3},{5,4},{6,5},{7,6},{0,7},{9,8},{10,9},{11,1... | collective-permute-start | bytes 1544 | tf_op jit(solution)/shard_map/ppermute | solution.py:19
  4.8 164.4 %collective-permute-start.5 = (f32[128]{0:T(128)S(1)}, f32[128]{0:T(128)S(1)}, u32[]{:S(2)}, u32[]{:S(2)}) collective-permute-start(f32[128]{0:T(128)S(1)} %get-tuple-element.159), channel_id=1, source_target_pairs={{0,1},{1,2},{2,3},{3,4},{4,5},{5,6},{6,7},{8,9},{9,10},{10,11},{11... | collective-permute-start | bytes 1544 | tf_op jit(solution)/shard_map/ppermute | solution.py:33
  6.3 162.6 %collective-permute-start.3 = (f32[512]{0:T(512)S(1)}, f32[512]{0:T(512)S(1)}, u32[]{:S(2)}, u32[]{:S(2)}) collective-permute-start(f32[512]{0:T(512)S(1)} %slice_reduce_fusion), channel_id=1, source_target_pairs={{0,8},{8,16},{16,24},{24,32},{32,40},{40,48},{48,56},{56,64},{64,7... | collective-permute-start | bytes 6152 | tf_op jit(solution)/shard_map/ppermute | solution.py:27
  175.6 79.0 %collective-permute-start.6 = (f32[1,128]{1,0:T(1,128)S(1)}, f32[1,128]{1,0:T(1,128)S(1)}, u32[]{:S(2)}, u32[]{:S(2)}) collective-permute-start(f32[1,128]{1,0:T(1,128)S(1)} %get-tuple-element.158), channel_id=1, source_target_pairs={{0,1},{1,2},{2,3},{3,4},{4,5},{5,6},{6,7},{7,0},{8,9},{9,10},{10,1... | collective-permute-start | bytes 1544 | tf_op jit(solution)/shard_map/ppermute | solution.py:16
  175.6 78.9 %collective-permute-start.7 = (f32[1,128]{1,0:T(1,128)S(1)}, f32[1,128]{1,0:T(1,128)S(1)}, u32[]{:S(2)}, u32[]{:S(2)}) collective-permute-start(f32[1,128]{1,0:T(1,128)S(1)} %get-tuple-element.157), channel_id=1, source_target_pairs={{1,0},{2,1},{3,2},{4,3},{5,4},{6,5},{7,6},{0,7},{9,8},{10,9},{11,1... | collective-permute-start | bytes 1544 | tf_op jit(solution)/shard_map/ppermute | solution.py:19
  266.1 78.6 %collective-permute-start.10 = (f32[1,128]{1,0:T(1,128)S(1)}, f32[1,128]{1,0:T(1,128)S(1)}, u32[]{:S(2)}, u32[]{:S(2)}) collective-permute-start(f32[1,128]{1,0:T(1,128)S(1)} %get-tuple-element.156), channel_id=1, source_target_pairs={{0,1},{1,2},{2,3},{3,4},{4,5},{5,6},{6,7},{7,0},{8,9},{9,10},{10,1... | collective-permute-start | bytes 1544 | tf_op jit(solution)/shard_map/ppermute | solution.py:16
  266.1 78.6 %collective-permute-start.11 = (f32[1,128]{1,0:T(1,128)S(1)}, f32[1,128]{1,0:T(1,128)S(1)}, u32[]{:S(2)}, u32[]{:S(2)}) collective-permute-start(f32[1,128]{1,0:T(1,128)S(1)} %get-tuple-element.155), channel_id=1, source_target_pairs={{1,0},{2,1},{3,2},{4,3},{5,4},{6,5},{7,6},{0,7},{9,8},{10,9},{11,1... | collective-permute-start | bytes 1544 | tf_op jit(solution)/shard_map/ppermute | solution.py:19
  357.2 78.6 %collective-permute-start.14 = (f32[1,128]{1,0:T(1,128)S(1)}, f32[1,128]{1,0:T(1,128)S(1)}, u32[]{:S(2)}, u32[]{:S(2)}) collective-permute-start(f32[1,128]{1,0:T(1,128)S(1)} %get-tuple-element.154), channel_id=1, source_target_pairs={{0,1},{1,2},{2,3},{3,4},{4,5},{5,6},{6,7},{7,0},{8,9},{9,10},{10,1... | collective-permute-start | bytes 1544 | tf_op jit(solution)/shard_map/ppermute | solution.py:16
  357.2 78.6 %collective-permute-start.15 = (f32[1,128]{1,0:T(1,128)S(1)}, f32[1,128]{1,0:T(1,128)S(1)}, u32[]{:S(2)}, u32[]{:S(2)}) collective-permute-start(f32[1,128]{1,0:T(1,128)S(1)} %get-tuple-element.153), channel_id=1, source_target_pairs={{1,0},{2,1},{3,2},{4,3},{5,4},{6,5},{7,6},{0,7},{9,8},{10,9},{11,1... | collective-permute-start | bytes 1544 | tf_op jit(solution)/shard_map/ppermute | solution.py:19
  438.7 8.5 collective-permute-start.16
  449.3 79.8 %collective-permute-start.18 = (f32[1,128]{1,0:T(1,128)S(1)}, f32[1,128]{1,0:T(1,128)S(1)}, u32[]{:S(2)}, u32[]{:S(2)}) collective-permute-start(f32[1,128]{1,0:T(1,128)S(1)} %get-tuple-element.152), channel_id=1, source_target_pairs={{0,1},{1,2},{2,3},{3,4},{4,5},{5,6},{6,7},{7,0},{8,9},{9,10},{10,1... | collective-permute-start | bytes 1544 | tf_op jit(solution)/shard_map/ppermute | solution.py:16
  449.3 79.8 %collective-permute-start.19 = (f32[1,128]{1,0:T(1,128)S(1)}, f32[1,128]{1,0:T(1,128)S(1)}, u32[]{:S(2)}, u32[]{:S(2)}) collective-permute-start(f32[1,128]{1,0:T(1,128)S(1)} %get-tuple-element.151), channel_id=1, source_target_pairs={{1,0},{2,1},{3,2},{4,3},{5,4},{6,5},{7,6},{0,7},{9,8},{10,9},{11,1... | collective-permute-start | bytes 1544 | tf_op jit(solution)/shard_map/ppermute | solution.py:19
  541.9 78.6 %collective-permute-start.22 = (f32[1,128]{1,0:T(1,128)S(1)}, f32[1,128]{1,0:T(1,128)S(1)}, u32[]{:S(2)}, u32[]{:S(2)}) collective-permute-start(f32[1,128]{1,0:T(1,128)S(1)} %get-tuple-element.150), channel_id=1, source_target_pairs={{0,1},{1,2},{2,3},{3,4},{4,5},{5,6},{6,7},{7,0},{8,9},{9,10},{10,1... | collective-permute-start | bytes 1544 | tf_op jit(solution)/shard_map/ppermute | solution.py:16
  542.0 78.6 %collective-permute-start.23 = (f32[1,128]{1,0:T(1,128)S(1)}, f32[1,128]{1,0:T(1,128)S(1)}, u32[]{:S(2)}, u32[]{:S(2)}) collective-permute-start(f32[1,128]{1,0:T(1,128)S(1)} %get-tuple-element.149), channel_id=1, source_target_pairs={{1,0},{2,1},{3,2},{4,3},{5,4},{6,5},{7,6},{0,7},{9,8},{10,9},{11,1... | collective-permute-start | bytes 1544 | tf_op jit(solution)/shard_map/ppermute | solution.py:19
  623.4 8.7 collective-permute-start.24
  633.4 78.6 %collective-permute-start.26 = (f32[1,128]{1,0:T(1,128)S(1)}, f32[1,128]{1,0:T(1,128)S(1)}, u32[]{:S(2)}, u32[]{:S(2)}) collective-permute-start(f32[1,128]{1,0:T(1,128)S(1)} %get-tuple-element.148), channel_id=1, source_target_pairs={{0,1},{1,2},{2,3},{3,4},{4,5},{5,6},{6,7},{7,0},{8,9},{9,10},{10,1... | collective-permute-start | bytes 1544 | tf_op jit(solution)/shard_map/ppermute | solution.py:16
  633.5 78.6 %collective-permute-start.27 = (f32[1,128]{1,0:T(1,128)S(1)}, f32[1,128]{1,0:T(1,128)S(1)}, u32[]{:S(2)}, u32[]{:S(2)}) collective-permute-start(f32[1,128]{1,0:T(1,128)S(1)} %get-tuple-element.147), channel_id=1, source_target_pairs={{1,0},{2,1},{3,2},{4,3},{5,4},{6,5},{7,6},{0,7},{9,8},{10,9},{11,1... | collective-permute-start | bytes 1544 | tf_op jit(solution)/shard_map/ppermute | solution.py:19
  715.9 8.6 collective-permute-start.28
  725.9 78.6 %collective-permute-start.30 = (f32[1,128]{1,0:T(1,128)S(1)}, f32[1,128]{1,0:T(1,128)S(1)}, u32[]{:S(2)}, u32[]{:S(2)}) collective-permute-start(f32[1,128]{1,0:T(1,128)S(1)} %get-tuple-element.146), channel_id=1, source_target_pairs={{0,1},{1,2},{2,3},{3,4},{4,5},{5,6},{6,7},{7,0},{8,9},{9,10},{10,1... | collective-permute-start | bytes 1544 | tf_op jit(solution)/shard_map/ppermute | solution.py:16
  725.9 78.6 %collective-permute-start.31 = (f32[1,128]{1,0:T(1,128)S(1)}, f32[1,128]{1,0:T(1,128)S(1)}, u32[]{:S(2)}, u32[]{:S(2)}) collective-permute-start(f32[1,128]{1,0:T(1,128)S(1)} %get-tuple-element.145), channel_id=1, source_target_pairs={{1,0},{2,1},{3,2},{4,3},{5,4},{6,5},{7,6},{0,7},{9,8},{10,9},{11,1... | collective-permute-start | bytes 1544 | tf_op jit(solution)/shard_map/ppermute | solution.py:19
  805.4 8.8 collective-permute-start.33
  807.3 8.6 collective-permute-start.32
  817.0 39.5 %all-to-all-start = ((f32[64,8,128]{2,1,0:T(8,128)}), f32[64,8,128]{2,1,0:T(8,128)S(1)}, u32[]{:S(2)}, u32[]{:S(2)}) async-start(f32[64,8,128]{2,1,0:T(8,128)} %fusion.9), calls=%async_computation | async-start | bytes 524288 | tf_op jit(solution)/shard_map/all_to_all | solution.py:137
  (14 other events, 106.4 us)
where the time goes:
time: 886 us; the launch traced here: 885 us
  blocking collectives  706 us (80%)
  starting transfers between devices  92.4 us (10%)
  waiting for transfers between devices  60.6 us (7%)
  other arithmetic  14.4 us (2%)
  local copies, waits for them, and re-layouts  10.2 us (1%)
    all_gather x9, blocking collectives, mirror_row(): gathered = lax.all_gather(values, 'lon', axis=0, tiled=True)  682 us
    ppermute x16, starting transfers between devices, with_halo(): lax.ppermute(lax.slice_in_dim(block, 0, width, axis=dim), axis, backward)  50.6 us
    all_to_all x1, blocking collectives, local(): lax.all_to_all(smoothed, 'lon', split_axis=1, concat_axis=0, tiled=True)  23.8 us
    all_to_all x1, waiting for transfers between devices, local(): lax.all_to_all(gradient, 'lon', split_axis=0, concat_axis=1, tiled=True)  21.2 us
    ppermute x16, waiting for transfers between devices, with_halo(): lax.ppermute(lax.slice_in_dim(block, block.shape[dim] - width, None, axis...  20.1 us
    ppermute x16, starting transfers between devices, with_halo(): lax.ppermute(lax.slice_in_dim(block, block.shape[dim] - width, None, axis...  19.8 us
    ppermute x16, waiting for transfers between devices, with_halo(): lax.ppermute(lax.slice_in_dim(block, 0, width, axis=dim), axis, backward)  19.4 us
  transfers between devices with their start and end apart: 35, of which 17 were waited for; matrix products, arithmetic and copies ran while one was open for 0% of the time, Pallas kernels for 0%

commit v1 on v0

--- a/solution.py
+++ b/solution.py
@@ -134,7 +134,16 @@
         carried = -adjoint
         adjoint = updated
     gradient = wet_frac * (adjoint + carried)
-    lines = lax.all_to_all(gradient, "lon", split_axis=0, concat_axis=1, tiled=True)
+    note_set = lambda patch, ax_name: jnp.concatenate(
+        lax.all_to_all(
+            jnp.stack(jnp.split(patch, lax.psum(1, axis_name=ax_name), axis=0), axis=0),
+            ax_name,
+            0,
+            0,
+        ),
+        axis=1,
+    )
+    lines = note_set(gradient, "lon")
     line_rows = row_count // lon_count
     row_scales = lax.dynamic_slice_in_dim(
         smooth_scale, lax.axis_index("lon") * line_rows, line_rows

time: 886 us -> 919 us (1.037)
  local copies, waits for them, and re-layouts: 10.2 us -> 48.1 us
    unnamed x8 -> x71, local copies, waits for them, and re-layouts: 0.74 us -> 38.1 us
where the time goes in v1:
time: 919 us; the launch traced here: 918 us
  blocking collectives  708 us (77%)
  starting transfers between devices  89 us (10%)
  waiting for transfers between devices  57.4 us (6%)
  local copies, waits for them, and re-layouts  48.1 us (5%)
  other arithmetic  13.7 us (1%)
    all_gather x9, blocking collectives, mirror_row(): gathered = lax.all_gather(values, 'lon', axis=0, tiled=True)  682 us
    ppermute x16, starting transfers between devices, with_halo(): lax.ppermute(lax.slice_in_dim(block, 0, width, axis=dim), axis, backward)  50.6 us
    unnamed x71, local copies, waits for them, and re-layouts  38.1 us
    all_to_all x1, blocking collectives, local(): lax.all_to_all(smoothed, 'lon', split_axis=1, concat_axis=0, tiled=True)  25.7 us
    ppermute x16, waiting for transfers between devices, with_halo(): lax.ppermute(lax.slice_in_dim(block, block.shape[dim] - width, None, axis...  19.8 us
    ppermute x16, starting transfers between devices, with_halo(): lax.ppermute(lax.slice_in_dim(block, block.shape[dim] - width, None, axis...  19.8 us
    ppermute x16, waiting for transfers between devices, with_halo(): lax.ppermute(lax.slice_in_dim(block, 0, width, axis=dim), axis, backward)  19.4 us
  transfers between devices with their start and end apart: 35, of which 17 were waited for; matrix products, arithmetic and copies ran while one was open for 0% of the time, Pallas kernels for 0%

profile of v1, /device:TPU:2, one launch (start us, length us, event | category | flops | bytes accessed | tf_op | source)
XLA Modules:
  0.0 917.7 jit_solution(13481285260757724309)
XLA Ops:
  6.3 3.4 collective-permute-start.3
  9.7 79.2 %all-gather = f32[1,8192]{1,0:T(1,128)S(1)} all-gather(f32[1,128]{1,0:T(1,128)S(1)} %get-tuple-element.190), channel_id=2, replica_groups=mesh['lon'=64,'lat'=8] {'lon'}, dimensions={1}, use_global_device_ids=true | all-gather | bytes 33280 | tf_op jit(solution)/shard_map/all_gather | solution.py:85
  89.1 72.9 %all-gather.1 = f32[1,8192]{1,0:T(1,128)S(1)} all-gather(f32[1,128]{1,0:T(1,128)S(1)} %get-tuple-element.192), channel_id=3, replica_groups=mesh['lon'=64,'lat'=8] {'lon'}, dimensions={1}, use_global_device_ids=true | all-gather | bytes 33280 | tf_op jit(solution)/shard_map/all_gather | solution.py:85
  175.6 2.9 collective-permute-start.7
  178.5 75.9 %all-gather.2 = f32[1,8192]{1,0:T(1,128)S(1)} all-gather(f32[1,128]{1,0:T(1,128)S(1)} %get-tuple-element.188), channel_id=4, replica_groups=mesh['lon'=64,'lat'=8] {'lon'}, dimensions={1}, use_global_device_ids=true | all-gather | bytes 33280 | tf_op jit(solution)/shard_map/all_gather | solution.py:85
  257.4 3.9 collective-permute-start.8
  269.0 75.5 %all-gather.3 = f32[1,8192]{1,0:T(1,128)S(1)} all-gather(f32[1,128]{1,0:T(1,128)S(1)} %get-tuple-element.186), channel_id=5, replica_groups=mesh['lon'=64,'lat'=8] {'lon'}, dimensions={1}, use_global_device_ids=true | all-gather | bytes 33280 | tf_op jit(solution)/shard_map/all_gather | solution.py:85
  345.5 3.0 collective-permute-start.13
  360.2 75.6 %all-gather.4 = f32[1,8192]{1,0:T(1,128)S(1)} all-gather(f32[1,128]{1,0:T(1,128)S(1)} %get-tuple-element.184), channel_id=6, replica_groups=mesh['lon'=64,'lat'=8] {'lon'}, dimensions={1}, use_global_device_ids=true | all-gather | bytes 33280 | tf_op jit(solution)/shard_map/all_gather | solution.py:85
  438.7 3.9 collective-permute-start.16
  449.3 3.0 collective-permute-start.19
  452.3 76.7 %all-gather.5 = f32[1,8192]{1,0:T(1,128)S(1)} all-gather(f32[1,128]{1,0:T(1,128)S(1)} %get-tuple-element.182), channel_id=7, replica_groups=mesh['lon'=64,'lat'=8] {'lon'}, dimensions={1}, use_global_device_ids=true | all-gather | bytes 33280 | tf_op jit(solution)/shard_map/all_gather | solution.py:85
  529.2 3.0 collective-permute-start.21
  537.5 3.1 collective-permute-done.20
  544.9 75.6 %all-gather.6 = f32[1,8192]{1,0:T(1,128)S(1)} all-gather(f32[1,128]{1,0:T(1,128)S(1)} %get-tuple-element.180), channel_id=8, replica_groups=mesh['lon'=64,'lat'=8] {'lon'}, dimensions={1}, use_global_device_ids=true | all-gather | bytes 33280 | tf_op jit(solution)/shard_map/all_gather | solution.py:85
  623.4 3.9 collective-permute-start.24
  636.4 75.5 %all-gather.7 = f32[1,8192]{1,0:T(1,128)S(1)} all-gather(f32[1,128]{1,0:T(1,128)S(1)} %get-tuple-element.178), channel_id=9, replica_groups=mesh['lon'=64,'lat'=8] {'lon'}, dimensions={1}, use_global_device_ids=true | all-gather | bytes 33280 | tf_op jit(solution)/shard_map/all_gather | solution.py:85
  712.9 3.0 collective-permute-start.29
  721.4 3.1 collective-permute-done.28
  728.8 75.6 %all-gather.8 = f32[1,8192]{1,0:T(1,128)S(1)} all-gather(f32[1,128]{1,0:T(1,128)S(1)} %get-tuple-element.176), channel_id=10, replica_groups=mesh['lon'=64,'lat'=8] {'lon'}, dimensions={1}, use_global_device_ids=true | all-gather | bytes 33280 | tf_op jit(solution)/shard_map/all_gather | solution.py:85
  807.3 3.9 collective-permute-start.32
  854.0 14.0 %all-to-all-start = ((f32[64,8,128]{2,1,0:T(8,128)}), f32[64,8,128]{2,1,0:T(8,128)S(1)}, u32[]{:S(2)}, u32[]{:S(2)}) async-start(f32[64,8,128]{2,1,0:T(8,128)} %constant_dynamic-update-slice_fusion), calls=%async_computation | async-start | bytes 524288 | tf_op jit(solution)/shard_map/all_to_all | solution.py:138
  869.0 18.3 %all-to-all-done = f32[64,8,128]{2,1,0:T(8,128)S(1)} async-done(((f32[64,8,128]{2,1,0:T(8,128)}), f32[64,8,128]{2,1,0:T(8,128)S(1)}, u32[]{:S(2)}, u32[]{:S(2)}) %all-to-all-start) | async-done | bytes 262176 | tf_op jit(solution)/shard_map/all_to_all | solution.py:138
  891.3 25.7 %all_to_all.21 = f32[8,64,128]{2,0,1:T(8,128)S(1)} all-to-all(f32[8,64,128]{2,0,1:T(8,128)S(1)} %copy.2507), channel_id=1, replica_groups=mesh['lon'=64,'lat'=8] {'lon'}, dimensions={1} | all-to-all | bytes 524288 | tf_op jit(solution)/shard_map/all_to_all | solution.py:157
  (259 shorter events, 136.1 us)
Async XLA Ops:
  1.8 160.3 %collective-permute-start = (f32[1,128]{1,0:T(1,128)S(1)}, f32[1,128]{1,0:T(1,128)S(1)}, u32[]{:S(2)}, u32[]{:S(2)}) collective-permute-start(f32[1,128]{1,0:T(1,128)S(1)} %get-tuple-element.192), channel_id=1, source_target_pairs={{0,1},{1,2},{2,3},{3,4},{4,5},{5,6},{6,7},{7,0},{8,9},{9,10},{10,1... | collective-permute-start | bytes 1544 | tf_op jit(solution)/shard_map/ppermute | solution.py:16
  1.8 160.3 %collective-permute-start.1 = (f32[1,128]{1,0:T(1,128)S(1)}, f32[1,128]{1,0:T(1,128)S(1)}, u32[]{:S(2)}, u32[]{:S(2)}) collective-permute-start(f32[1,128]{1,0:T(1,128)S(1)} %get-tuple-element.191), channel_id=1, source_target_pairs={{1,0},{2,1},{3,2},{4,3},{5,4},{6,5},{7,6},{0,7},{9,8},{10,9},{11,1... | collective-permute-start | bytes 1544 | tf_op jit(solution)/shard_map/ppermute | solution.py:19
  4.8 164.4 %collective-permute-start.5 = (f32[128]{0:T(128)S(1)}, f32[128]{0:T(128)S(1)}, u32[]{:S(2)}, u32[]{:S(2)}) collective-permute-start(f32[128]{0:T(128)S(1)} %get-tuple-element.189), channel_id=1, source_target_pairs={{0,1},{1,2},{2,3},{3,4},{4,5},{5,6},{6,7},{8,9},{9,10},{10,11},{11... | collective-permute-start | bytes 1544 | tf_op jit(solution)/shard_map/ppermute | solution.py:33
  6.3 162.6 %collective-permute-start.3 = (f32[512]{0:T(512)S(1)}, f32[512]{0:T(512)S(1)}, u32[]{:S(2)}, u32[]{:S(2)}) collective-permute-start(f32[512]{0:T(512)S(1)} %slice_reduce_fusion), channel_id=1, source_target_pairs={{0,8},{8,16},{16,24},{24,32},{32,40},{40,48},{48,56},{56,64},{64,7... | collective-permute-start | bytes 6152 | tf_op jit(solution)/shard_map/ppermute | solution.py:27
  163.0 8.5 collective-permute-start.4
  175.6 79.0 %collective-permute-start.6 = (f32[1,128]{1,0:T(1,128)S(1)}, f32[1,128]{1,0:T(1,128)S(1)}, u32[]{:S(2)}, u32[]{:S(2)}) collective-permute-start(f32[1,128]{1,0:T(1,128)S(1)} %get-tuple-element.188), channel_id=1, source_target_pairs={{0,1},{1,2},{2,3},{3,4},{4,5},{5,6},{6,7},{7,0},{8,9},{9,10},{10,1... | collective-permute-start | bytes 1544 | tf_op jit(solution)/shard_map/ppermute | solution.py:16
  175.6 78.9 %collective-permute-start.7 = (f32[1,128]{1,0:T(1,128)S(1)}, f32[1,128]{1,0:T(1,128)S(1)}, u32[]{:S(2)}, u32[]{:S(2)}) collective-permute-start(f32[1,128]{1,0:T(1,128)S(1)} %get-tuple-element.187), channel_id=1, source_target_pairs={{1,0},{2,1},{3,2},{4,3},{5,4},{6,5},{7,6},{0,7},{9,8},{10,9},{11,1... | collective-permute-start | bytes 1544 | tf_op jit(solution)/shard_map/ppermute | solution.py:19
  266.1 78.6 %collective-permute-start.10 = (f32[1,128]{1,0:T(1,128)S(1)}, f32[1,128]{1,0:T(1,128)S(1)}, u32[]{:S(2)}, u32[]{:S(2)}) collective-permute-start(f32[1,128]{1,0:T(1,128)S(1)} %get-tuple-element.186), channel_id=1, source_target_pairs={{0,1},{1,2},{2,3},{3,4},{4,5},{5,6},{6,7},{7,0},{8,9},{9,10},{10,1... | collective-permute-start | bytes 1544 | tf_op jit(solution)/shard_map/ppermute | solution.py:16
  266.1 78.6 %collective-permute-start.11 = (f32[1,128]{1,0:T(1,128)S(1)}, f32[1,128]{1,0:T(1,128)S(1)}, u32[]{:S(2)}, u32[]{:S(2)}) collective-permute-start(f32[1,128]{1,0:T(1,128)S(1)} %get-tuple-element.185), channel_id=1, source_target_pairs={{1,0},{2,1},{3,2},{4,3},{5,4},{6,5},{7,6},{0,7},{9,8},{10,9},{11,1... | collective-permute-start | bytes 1544 | tf_op jit(solution)/shard_map/ppermute | solution.py:19
  345.5 8.5 collective-permute-start.13
  357.2 78.6 %collective-permute-start.14 = (f32[1,128]{1,0:T(1,128)S(1)}, f32[1,128]{1,0:T(1,128)S(1)}, u32[]{:S(2)}, u32[]{:S(2)}) collective-permute-start(f32[1,128]{1,0:T(1,128)S(1)} %get-tuple-element.184), channel_id=1, source_target_pairs={{0,1},{1,2},{2,3},{3,4},{4,5},{5,6},{6,7},{7,0},{8,9},{9,10},{10,1... | collective-permute-start | bytes 1544 | tf_op jit(solution)/shard_map/ppermute | solution.py:16
  357.2 78.6 %collective-permute-start.15 = (f32[1,128]{1,0:T(1,128)S(1)}, f32[1,128]{1,0:T(1,128)S(1)}, u32[]{:S(2)}, u32[]{:S(2)}) collective-permute-start(f32[1,128]{1,0:T(1,128)S(1)} %get-tuple-element.183), channel_id=1, source_target_pairs={{1,0},{2,1},{3,2},{4,3},{5,4},{6,5},{7,6},{0,7},{9,8},{10,9},{11,1... | collective-permute-start | bytes 1544 | tf_op jit(solution)/shard_map/ppermute | solution.py:19
  438.7 8.5 collective-permute-start.16
  449.3 79.8 %collective-permute-start.18 = (f32[1,128]{1,0:T(1,128)S(1)}, f32[1,128]{1,0:T(1,128)S(1)}, u32[]{:S(2)}, u32[]{:S(2)}) collective-permute-start(f32[1,128]{1,0:T(1,128)S(1)} %get-tuple-element.182), channel_id=1, source_target_pairs={{0,1},{1,2},{2,3},{3,4},{4,5},{5,6},{6,7},{7,0},{8,9},{9,10},{10,1... | collective-permute-start | bytes 1544 | tf_op jit(solution)/shard_map/ppermute | solution.py:16
  449.3 79.8 %collective-permute-start.19 = (f32[1,128]{1,0:T(1,128)S(1)}, f32[1,128]{1,0:T(1,128)S(1)}, u32[]{:S(2)}, u32[]{:S(2)}) collective-permute-start(f32[1,128]{1,0:T(1,128)S(1)} %get-tuple-element.181), channel_id=1, source_target_pairs={{1,0},{2,1},{3,2},{4,3},{5,4},{6,5},{7,6},{0,7},{9,8},{10,9},{11,1... | collective-permute-start | bytes 1544 | tf_op jit(solution)/shard_map/ppermute | solution.py:19
  541.9 78.6 %collective-permute-start.22 = (f32[1,128]{1,0:T(1,128)S(1)}, f32[1,128]{1,0:T(1,128)S(1)}, u32[]{:S(2)}, u32[]{:S(2)}) collective-permute-start(f32[1,128]{1,0:T(1,128)S(1)} %get-tuple-element.180), channel_id=1, source_target_pairs={{0,1},{1,2},{2,3},{3,4},{4,5},{5,6},{6,7},{7,0},{8,9},{9,10},{10,1... | collective-permute-start | bytes 1544 | tf_op jit(solution)/shard_map/ppermute | solution.py:16
  542.0 78.6 %collective-permute-start.23 = (f32[1,128]{1,0:T(1,128)S(1)}, f32[1,128]{1,0:T(1,128)S(1)}, u32[]{:S(2)}, u32[]{:S(2)}) collective-permute-start(f32[1,128]{1,0:T(1,128)S(1)} %get-tuple-element.179), channel_id=1, source_target_pairs={{1,0},{2,1},{3,2},{4,3},{5,4},{6,5},{7,6},{0,7},{9,8},{10,9},{11,1... | collective-permute-start | bytes 1544 | tf_op jit(solution)/shard_map/ppermute | solution.py:19
  623.4 8.7 collective-permute-start.24
  633.4 78.6 %collective-permute-start.26 = (f32[1,128]{1,0:T(1,128)S(1)}, f32[1,128]{1,0:T(1,128)S(1)}, u32[]{:S(2)}, u32[]{:S(2)}) collective-permute-start(f32[1,128]{1,0:T(1,128)S(1)} %get-tuple-element.178), channel_id=1, source_target_pairs={{0,1},{1,2},{2,3},{3,4},{4,5},{5,6},{6,7},{7,0},{8,9},{9,10},{10,1... | collective-permute-start | bytes 1544 | tf_op jit(solution)/shard_map/ppermute | solution.py:16
  633.5 78.6 %collective-permute-start.27 = (f32[1,128]{1,0:T(1,128)S(1)}, f32[1,128]{1,0:T(1,128)S(1)}, u32[]{:S(2)}, u32[]{:S(2)}) collective-permute-start(f32[1,128]{1,0:T(1,128)S(1)} %get-tuple-element.177), channel_id=1, source_target_pairs={{1,0},{2,1},{3,2},{4,3},{5,4},{6,5},{7,6},{0,7},{9,8},{10,9},{11,1... | collective-permute-start | bytes 1544 | tf_op jit(solution)/shard_map/ppermute | solution.py:19
  715.9 8.6 collective-permute-start.28
  725.9 78.6 %collective-permute-start.30 = (f32[1,128]{1,0:T(1,128)S(1)}, f32[1,128]{1,0:T(1,128)S(1)}, u32[]{:S(2)}, u32[]{:S(2)}) collective-permute-start(f32[1,128]{1,0:T(1,128)S(1)} %get-tuple-element.176), channel_id=1, source_target_pairs={{0,1},{1,2},{2,3},{3,4},{4,5},{5,6},{6,7},{7,0},{8,9},{9,10},{10,1... | collective-permute-start | bytes 1544 | tf_op jit(solution)/shard_map/ppermute | solution.py:16
  725.9 78.6 %collective-permute-start.31 = (f32[1,128]{1,0:T(1,128)S(1)}, f32[1,128]{1,0:T(1,128)S(1)}, u32[]{:S(2)}, u32[]{:S(2)}) collective-permute-start(f32[1,128]{1,0:T(1,128)S(1)} %get-tuple-element.175), channel_id=1, source_target_pairs={{1,0},{2,1},{3,2},{4,3},{5,4},{6,5},{7,6},{0,7},{9,8},{10,9},{11,1... | collective-permute-start | bytes 1544 | tf_op jit(solution)/shard_map/ppermute | solution.py:19
  854.0 33.2 %all-to-all-start = ((f32[64,8,128]{2,1,0:T(8,128)}), f32[64,8,128]{2,1,0:T(8,128)S(1)}, u32[]{:S(2)}, u32[]{:S(2)}) async-start(f32[64,8,128]{2,1,0:T(8,128)} %constant_dynamic-update-slice_fusion), calls=%async_computation | async-start | bytes 524288 | tf_op jit(solution)/shard_map/all_to_all | solution.py:138
  (14 other events, 106.2 us)
